TPU v7x, 128 devices: a whole 4x4x4 slice. The times are simulated.
128 devices in a mesh: seq: 8 (over z, y_hi), chan: 8 (over x, core), dp: 2 (over y_lo).
Axes of the slice: x: 4, y: 4 (y_hi: 2, y_lo: 2; y = y_hi * 2 + y_lo), z: 4, core: 2. Of those that a mesh axis runs over, the one named last changes fastest.
Arguments:
- tokens: bfloat16 [2, 1024, 8192], P('dp', 'seq'), may hold values from -6 to 6
- in_weight: bfloat16 [8192, 3, 4096], P('seq', None, 'chan'), may hold values from -0.0625 to 0.0625
- short_taps: float32 [3, 3, 4096], P(None, None, 'chan'), may hold values from -1 to 1
- long_filter: float32 [1024, 4096], P('seq', 'chan'), may hold values from -1.25 to 1.25
- skip_gain: float32 [4096], P('chan'), may hold values from 0.5 to 1.5
- cotangent: bfloat16 [2, 1024, 4096], P('dp', 'seq', 'chan'), may hold values from -6 to 6
Outputs:
- hyena_out: bfloat16 [2, 1024, 4096], P('dp', 'seq', 'chan')
- grad_tokens: bfloat16 [2, 1024, 8192], P('dp', None, ('seq', 'chan'))
- grad_weight: bfloat16 [8192, 3, 4096], P('seq', None, 'chan')
- grad_filter: float32 [1024, 4096], P('seq', 'chan')
All inputs are finite; a program needn't handle non-finite values.
Results may differ from a plain program's by a relative error of at most 0.02.
Values may be sent and summed in bfloat16 or wider, within the bound.
No kernel may reach another device: no remote copies, remote signals or barrier semaphores. Data moves between devices by JAX's collectives and lax.ppermute only.
A program may use at most 128 MiB of HBM per device.

v0:
```python
import math
import jax
import jax.numpy as jnp
from jax import lax
from jax.sharding import PartitionSpec as P


def partner_2(shard, axis, stride):
    return lax.ppermute(shard, axis, [(i, i ^ 1 << stride) for i in range(lax.axis_size(axis))])


def shifted(value, axis, steps):
    count = lax.axis_size(axis)
    leading, last = (max(0, -steps), min(count, count - steps))
    return lax.ppermute(value, axis, [(source, source + steps) for source in range(leading, last)])


def complex_mul(left, right):
    return jnp.stack(
        [left[0] * right[0] - left[1] * right[1], left[0] * right[1] + left[1] * right[0]]
    )


def conjugate(signal):
    return jnp.stack([signal[0], -signal[1]])


def dft_tables(length):
    index = jnp.arange(length, dtype=jnp.int32)
    product = index[:, None] * index[None, :] % length
    phases = 2.0 * math.pi / length * product.astype(jnp.float32)
    return (jnp.cos(phases), jnp.sin(phases))


def table_apply(cos_table, sin_table, sign, signal, form):
    high = lax.Precision.HIGHEST
    real_cos = jnp.einsum(form, cos_table, signal[0], precision=high)
    imag_cos = jnp.einsum(form, cos_table, signal[1], precision=high)
    real_sin = jnp.einsum(form, sin_table, signal[0], precision=high)
    imag_sin = jnp.einsum(form, sin_table, signal[1], precision=high)
    return jnp.stack([real_cos - sign * imag_sin, imag_cos + sign * real_sin])


def reverse_bits(seq_pos, seq_count):
    bit_total = seq_count.bit_length() - 1
    result = jnp.zeros((), jnp.int32)
    for bit_pos in range(bit_total):
        result = result + seq_pos // (1 << bit_pos) % 2 * (1 << bit_total - 1 - bit_pos)
    return result


def pairs_forward(signal, seq_count, seq_pos):
    bit_total = seq_count.bit_length() - 1
    for bit_pos in reversed(range(bit_total)):
        half_span = 1 << bit_pos
        partner = partner_2(signal, "seq", bit_pos)
        offset = (seq_pos % half_span).astype(jnp.float32)
        phases = -math.pi * offset / half_span
        twiddle = jnp.stack([jnp.cos(phases), jnp.sin(phases)])
        is_upper = seq_pos // half_span % 2 == 1
        signal = jnp.where(is_upper, complex_mul(partner - signal, twiddle), signal + partner)
    return signal


def pairs_inverse(signal, seq_count, seq_pos):
    bit_total = seq_count.bit_length() - 1
    for bit_pos in range(bit_total):
        half_span = 1 << bit_pos
        partner = partner_2(signal.astype(jnp.bfloat16), "seq", bit_pos).astype(signal.dtype)
        offset = (seq_pos % half_span).astype(jnp.float32)
        phases = math.pi * offset / half_span
        twiddle = jnp.stack([jnp.cos(phases), jnp.sin(phases)])
        is_upper = seq_pos // half_span % 2 == 1
        signal = jnp.where(
            is_upper, partner - complex_mul(signal, twiddle), signal + complex_mul(partner, twiddle)
        )
    return signal


def position_twiddle(spec_order, tok_rows, full_len, sign):
    k_index = 2 * spec_order + jnp.arange(2, dtype=jnp.int32)
    pos_rows = jnp.arange(tok_rows, dtype=jnp.int32)
    product = k_index[:, None] * pos_rows[None, :] % full_len
    phases = sign * 2.0 * math.pi / full_len * product.astype(jnp.float32)
    return jnp.stack([jnp.cos(phases), jnp.sin(phases)])[:, None, :, :, None]


def forward_spectrum(rows_in, seq_count, seq_pos):
    tok_rows = rows_in.shape[1]
    full_len = 2 * seq_count * tok_rows
    phase_shift = math.pi * seq_pos.astype(jnp.float32) / seq_count
    real_part = jnp.stack([rows_in, rows_in * jnp.cos(phase_shift)], axis=1)
    imag_part = jnp.stack([jnp.zeros_like(rows_in), -rows_in * jnp.sin(phase_shift)], axis=1)
    signal = jnp.stack([real_part, imag_part])
    signal = pairs_forward(signal, seq_count, seq_pos)
    spec_order = reverse_bits(seq_pos, seq_count)
    signal = complex_mul(signal, position_twiddle(spec_order, tok_rows, full_len, -1.0))
    cos_table, sin_table = dft_tables(tok_rows)
    return table_apply(cos_table, sin_table, -1.0, signal, "ka,gbac->gbkc")


def inverse_spectrum(signal, seq_count, seq_pos):
    tok_rows = signal.shape[3]
    full_len = 2 * seq_count * tok_rows
    cos_table, sin_table = dft_tables(tok_rows)
    signal = table_apply(cos_table, sin_table, 1.0, signal, "ka,gbac->gbkc")
    spec_order = reverse_bits(seq_pos, seq_count)
    signal = complex_mul(signal, position_twiddle(spec_order, tok_rows, full_len, 1.0))
    signal = pairs_inverse(signal, seq_count, seq_pos)
    phase_shift = math.pi * seq_pos.astype(jnp.float32) / seq_count
    combined = (
        signal[0][:, 0]
        + jnp.cos(phase_shift) * signal[0][:, 1]
        - jnp.sin(phase_shift) * signal[1][:, 1]
    )
    return combined / full_len


def local(tokens, in_weight, short_taps, long_filter, skip_gain, cotangent):
    seq_count = lax.axis_size("seq")
    seq_pos = lax.axis_index("seq")
    tok_rows = tokens.shape[1]
    slab_rows = in_weight.shape[0]
    chan_cols = in_weight.shape[2]
    taps_len = short_taps.shape[1]
    grad_scale = 1.0 / math.sqrt(lax.axis_size("dp") * seq_count * tok_rows)
    spread = lax.all_to_all(tokens[0], "seq", split_axis=1, concat_axis=0, tiled=True)
    flat_weight = in_weight.reshape(slab_rows, 3 * chan_cols)
    projected = lax.psum_scatter(
        jnp.dot(spread, flat_weight, preferred_element_type=jnp.float32),
        "seq",
        scatter_dimension=0,
        tiled=True,
    ).reshape(tok_rows, 3, chan_cols)
    rim_rows = shifted(projected[tok_rows - (taps_len - 1) :], "seq", 1)
    extended = jnp.concatenate([rim_rows, projected], axis=0)
    streams = jnp.zeros_like(projected)
    for tap_pos in range(taps_len):
        begin = taps_len - 1 - tap_pos
        streams = streams + short_taps[:, tap_pos, :] * extended[begin : begin + tok_rows]
    queries = streams[:, 0]
    keys_in = streams[:, 1]
    values_in = streams[:, 2]
    gated_in = keys_in * values_in
    spectra = forward_spectrum(jnp.stack([gated_in, long_filter]), seq_count, seq_pos)
    gated_freq = spectra[:, 0:1]
    filter_freq = spectra[:, 1:2]
    conv_out = (
        inverse_spectrum(complex_mul(gated_freq, filter_freq), seq_count, seq_pos)[0]
        + skip_gain * gated_in
    )
    hyena_out = (queries * conv_out).astype(jnp.bfloat16)[None]
    grad_in = cotangent[0].astype(jnp.float32)
    d_conv = grad_in * queries
    d_query = grad_in * conv_out
    conv_freq = forward_spectrum(d_conv[None], seq_count, seq_pos)
    pair_freq = jnp.concatenate(
        [
            complex_mul(conjugate(filter_freq), conv_freq),
            complex_mul(conjugate(gated_freq), conv_freq),
        ],
        axis=1,
    )
    back_rows = inverse_spectrum(pair_freq, seq_count, seq_pos)
    d_gated = back_rows[0] + skip_gain * d_conv
    filter_part = back_rows[1] * grad_scale
    d_streams = jnp.stack([d_query, d_gated * values_in, d_gated * keys_in], axis=1)
    rim_next = shifted(d_streams[: taps_len - 1], "seq", -1)
    ext_next = jnp.concatenate([d_streams, rim_next], axis=0)
    d_projected = jnp.zeros_like(d_streams)
    for tap_pos in range(taps_len):
        d_projected = (
            d_projected + short_taps[:, tap_pos, :] * ext_next[tap_pos : tap_pos + tok_rows]
        )
    d_projected = d_projected.astype(jnp.bfloat16).reshape(tok_rows, 3 * chan_cols)
    shard_rows = lax.all_gather(d_projected, "seq", axis=0, tiled=True)
    weight_total = lax.dot_general(
        spread, shard_rows, (((0,), (0,)), ((), ())), preferred_element_type=jnp.float32
    )
    token_block = lax.dot_general(
        shard_rows, flat_weight, (((1,), (1,)), ((), ())), preferred_element_type=jnp.float32
    )
    grad_tokens = lax.psum_scatter(
        token_block.astype(jnp.bfloat16), "chan", scatter_dimension=1, tiled=True
    )[None]
    weight_sum, filter_sum = (
        lax.psum((weight_total * grad_scale).astype(jnp.bfloat16), "dp").astype(jnp.float32),
        lax.psum(filter_part.astype(jnp.bfloat16), "dp").astype(jnp.float32),
    )
    grad_weight = weight_sum.astype(jnp.bfloat16).reshape(slab_rows, 3, chan_cols)
    return (hyena_out, grad_tokens, grad_weight, filter_sum)


def solution(mesh):
    placed = (
        P("dp", "seq", None),
        P("seq", None, "chan"),
        P(None, None, "chan"),
        P("seq", "chan"),
        P("chan"),
        P("dp", "seq", "chan"),
    )
    return jax.shard_map(
        local,
        mesh=mesh,
        in_specs=placed,
        out_specs=(
            P("dp", "seq", "chan"),
            P("dp", None, ("seq", "chan")),
            P("seq", None, "chan"),
            P("seq", "chan"),
        ),
        check_vma=False,
    )
```

profile of v0, /device:TPU:0, one launch (start us, length us, event | category | flops | bytes accessed | tf_op | source)
XLA Modules:
  0.0 742.5 jit_solution(11029934226150978450)
XLA Ops:
  7.2 4.1 copy.90
  11.3 8.0 %all-to-all-start = ((bf16[128,8,1024]{0,2,1:T(8,128)(2,1)}), bf16[128,8,1024]{0,2,1:T(8,128)(2,1)S(1)}, u32[]{:S(2)}, u32[]{:S(2)}) async-start(bf16[128,8,1024]{0,2,1:T(8,128)(2,1)} %bitcast.318), calls=%async_computation | async-start | bytes 4194304 | tf_op jit(solution)/shard_map/all_to_all | solution.py:127
  19.3 4.6 copy.92
  24.0 23.8 %all-to-all-done = bf16[128,8,1024]{0,2,1:T(8,128)(2,1)S(1)} async-done(((bf16[128,8,1024]{0,2,1:T(8,128)(2,1)}), bf16[128,8,1024]{0,2,1:T(8,128)(2,1)S(1)}, u32[]{:S(2)}, u32[]{:S(2)}) %all-to-all-start) | async-done | bytes 2097184 | tf_op jit(solution)/shard_map/all_to_all | solution.py:127
  47.8 2.6 copy.91
  50.4 8.6 %fusion.204 = f32[1024,1536]{1,0:T(8,128)} fusion(bf16[1024,1024]{1,0:T(8,128)(2,1)} %bitcast.327, bf16[1024,1536]{0,1:T(8,128)(2,1)} %bitcast.323), kind=kOutput, calls=%fused_computation.316 | convolution fusion | flops 3221225472 | bytes 11534336 | tf_op jit(solution)/shard_map/dot_general | solution.py:130
  59.7 95.1 %reduce-scatter.5.cloned.1.call-done = f32[128,1536]{1,0:T(8,128)} async-done(((f32[1024,1536]{1,0:T(8,128)}), f32[128,1536]{1,0:T(8,128)}) %reduce-scatter.5.cloned.1.call-update) | async-done | bytes 786448 | tf_op jit(solution)/shard_map/reduce_scatter | solution.py:129
  155.7 2.4 collective-permute-start
  158.3 1.4 copy.93
  161.0 1.7 pad_maximum_fusion
  162.6 4.8 collective-permute-start.1
  167.7 44.0 %collective-permute-done.1 = f32[2,2,2,128,512]{4,3,1,2,0:T(8,128)} collective-permute-done((f32[2,2,2,128,512]{4,3,1,2,0:T(8,128)}, f32[2,2,2,128,512]{4,3,1,2,0:T(8,128)}, u32[]{:S(2)}, u32[]{:S(2)}) %collective-permute-start.1) | collective-permute-done | bytes 2097184 | tf_op jit(solution)/shard_map/ppermute | solution.py:9
  211.6 2.1 fusion.183
  214.0 4.5 maximum_select_fusion
  218.5 2.0 collective-permute-start.2
  220.7 43.1 %collective-permute-done.2 = f32[2,2,2,128,512]{4,3,1,2,0:T(8,128)} collective-permute-done((f32[2,2,2,128,512]{4,3,1,2,0:T(8,128)}, f32[2,2,2,128,512]{4,3,1,2,0:T(8,128)}, u32[]{:S(2)}, u32[]{:S(2)}) %collective-permute-start.2) | collective-permute-done | bytes 2097184 | tf_op jit(solution)/shard_map/ppermute | solution.py:9
  263.8 3.8 fusion.212
  269.1 4.9 maximum_select_fusion.1
  274.0 2.2 collective-permute-start.3
  276.4 43.6 %collective-permute-done.3 = f32[2,2,2,128,512]{4,3,1,2,0:T(8,128)S(1)} collective-permute-done((f32[2,2,2,128,512]{4,3,1,2,0:T(8,128)}, f32[2,2,2,128,512]{4,3,1,2,0:T(8,128)S(1)}, u32[]{:S(2)}, u32[]{:S(2)}) %collective-permute-start.3) | collective-permute-done | bytes 2097184 | tf_op jit(solution)/shard_map/ppermute | solution.py:9
  319.9 2.1 sub.247
  322.2 2.4 maximum_select_fusion.2
  324.9 1.9 fusion.30
  326.9 1.9 fusion.26
  328.8 2.0 fusion.7
  330.8 2.0 fusion.5
  334.7 1.1 fusion.12
  337.0 2.2 collective-permute-start.4
  339.2 8.7 %collective-permute-done.4 = bf16[2,1,2,128,512]{4,3,2,1,0:T(8,128)(2,1)S(1)} collective-permute-done((bf16[2,1,2,128,512]{4,3,2,1,0:T(8,128)(2,1)S(1)}, bf16[2,1,2,128,512]{4,3,2,1,0:T(8,128)(2,1)S(1)}, u32[]{:S(2)}, u32[]{:S(2)}) %collective-permute-start.4) | collective-permute-done | bytes 524320 | tf_op jit(solution)/shard_map/ppermute | solution.py:9
  348.7 1.8 collective-permute-start.5
  350.7 8.8 %collective-permute-done.5 = bf16[2,1,2,128,512]{4,3,2,1,0:T(8,128)(2,1)S(1)} collective-permute-done((bf16[2,1,2,128,512]{4,3,2,1,0:T(8,128)(2,1)S(1)}, bf16[2,1,2,128,512]{4,3,2,1,0:T(8,128)(2,1)S(1)}, u32[]{:S(2)}, u32[]{:S(2)}) %collective-permute-start.5) | collective-permute-done | bytes 524320 | tf_op jit(solution)/shard_map/ppermute | solution.py:9
  359.8 1.2 fusion.189
  362.4 10.9 %collective-permute-done.6 = bf16[2,1,2,128,512]{4,3,2,1,0:T(8,128)(2,1)S(1)} collective-permute-done((bf16[2,1,2,128,512]{4,3,2,1,0:T(8,128)(2,1)}, bf16[2,1,2,128,512]{4,3,2,1,0:T(8,128)(2,1)S(1)}, u32[]{:S(2)}, u32[]{:S(2)}) %collective-permute-start.6) | collective-permute-done | bytes 524320 | tf_op jit(solution)/shard_map/ppermute | solution.py:9
  375.9 23.1 %collective-permute-done.7 = f32[2,1,2,128,512]{4,3,2,1,0:T(8,128)S(1)} collective-permute-done((f32[2,1,2,128,512]{4,3,2,1,0:T(8,128)S(1)}, f32[2,1,2,128,512]{4,3,2,1,0:T(8,128)S(1)}, u32[]{:S(2)}, u32[]{:S(2)}) %collective-permute-start.7) | collective-permute-done | bytes 1048608 | tf_op jit(solution)/shard_map/ppermute | solution.py:9
  399.7 2.9 collective-permute-start.8
  402.6 12.8 %collective-permute-done.8 = f32[2,1,2,128,512]{4,3,2,1,0:T(8,128)S(1)} collective-permute-done((f32[2,1,2,128,512]{4,3,2,1,0:T(8,128)S(1)}, f32[2,1,2,128,512]{4,3,2,1,0:T(8,128)S(1)}, u32[]{:S(2)}, u32[]{:S(2)}) %collective-permute-start.8) | collective-permute-done | bytes 1048608 | tf_op jit(solution)/shard_map/ppermute | solution.py:9
  416.7 4.4 collective-permute-start.9
  421.1 12.8 %collective-permute-done.9 = f32[2,1,2,128,512]{4,3,2,1,0:T(8,128)S(1)} collective-permute-done((f32[2,1,2,128,512]{4,3,2,1,0:T(8,128)S(1)}, f32[2,1,2,128,512]{4,3,2,1,0:T(8,128)S(1)}, u32[]{:S(2)}, u32[]{:S(2)}) %collective-permute-start.9) | collective-permute-done | bytes 1048608 | tf_op jit(solution)/shard_map/ppermute | solution.py:9
  435.0 1.2 fusion.75
  436.2 1.2 fusion.74
  437.4 1.2 fusion.11
  438.6 1.3 fusion.49
  440.2 1.3 fusion.20
  441.5 1.3 fusion.24
  442.8 1.3 convolution_add_fusion
  444.2 1.6 fusion.19
  446.0 3.8 collective-permute-start.10
  450.0 12.6 %collective-permute-done.10 = bf16[2,2,2,128,512]{4,3,1,2,0:T(8,128)(2,1)S(1)} collective-permute-done((bf16[2,2,2,128,512]{4,3,1,2,0:T(8,128)(2,1)S(1)}, bf16[2,2,2,128,512]{4,3,1,2,0:T(8,128)(2,1)S(1)}, u32[]{:S(2)}, u32[]{:S(2)}) %collective-permute-start.10) | collective-permute-done | bytes 1048608 | tf_op jit(solution)/shard_map/ppermute | solution.py:9
  464.1 2.1 collective-permute-start.11
  466.6 12.4 %collective-permute-done.11 = bf16[2,2,2,128,512]{4,3,1,2,0:T(8,128)(2,1)S(1)} collective-permute-done((bf16[2,2,2,128,512]{4,3,1,2,0:T(8,128)(2,1)S(1)}, bf16[2,2,2,128,512]{4,3,1,2,0:T(8,128)(2,1)S(1)}, u32[]{:S(2)}, u32[]{:S(2)}) %collective-permute-start.11) | collective-permute-done | bytes 1048608 | tf_op jit(solution)/shard_map/ppermute | solution.py:9
  480.5 17.3 %collective-permute-start.12 = (bf16[2,2,2,128,512]{4,3,1,2,0:T(8,128)(2,1)S(1)}, bf16[2,2,2,128,512]{4,3,1,2,0:T(8,128)(2,1)S(1)}, u32[]{:S(2)}, u32[]{:S(2)}) collective-permute-start(bf16[2,2,2,128,512]{4,3,1,2,0:T(8,128)(2,1)S(1)} %get-tuple-element.8), channel_id=1, source_target_pairs={{0,64},{16,80},{32,96},{48,112},{64,0},{80,16},{96,32},{112,48},{1... | collective-permute-start | bytes 3145736 | tf_op jit(solution)/shard_map/ppermute | solution.py:9
  498.2 12.5 %collective-permute-done.12 = bf16[2,2,2,128,512]{4,3,1,2,0:T(8,128)(2,1)S(1)} collective-permute-done((bf16[2,2,2,128,512]{4,3,1,2,0:T(8,128)(2,1)S(1)}, bf16[2,2,2,128,512]{4,3,1,2,0:T(8,128)(2,1)S(1)}, u32[]{:S(2)}, u32[]{:S(2)}) %collective-permute-start.12) | collective-permute-done | bytes 1048608 | tf_op jit(solution)/shard_map/ppermute | solution.py:9
  512.8 1.3 collective-permute-start.13
  514.1 5.8 collective-permute-done.13
  521.9 65.9 %all-gather.2.cloned.1.call-done = bf16[1024,1536]{0,1:T(8,128)(2,1)} async-done(((bf16[128,1536]{0,1:T(8,128)(2,1)}), bf16[1024,1536]{0,1:T(8,128)(2,1)}) %all-gather.2.cloned.1.call-update) | async-done | bytes 3145744 | tf_op jit(solution)/shard_map/all_gather | solution.py:176
  587.8 6.8 multiply_convert_fusion
  594.6 4.7 copy.118
  599.6 6.3 convolution_convert_fusion
  605.9 2.6 copy.149
  608.5 84.1 %all-reduce.5.cloned.1.call-done = (bf16[1024,3,512]{2,0,1:T(8,128)(2,1)}, bf16[128,512]{1,0:T(8,128)(2,1)}) async-done(((bf16[1024,3,512]{2,0,1:T(8,128)(2,1)}, bf16[128,512]{1,0:T(8,128)(2,1)}), (bf16[1024,3,512]{2,0,1:T(8,128)(2,1)}, bf16[128,512]{1,0:T(8,128)(2,1)})) %all-reduce.5.cloned.1.call-update) | async-done | bytes 3276816 | tf_op jit(solution)/shard_map/psum | solution.py:187
  692.6 1.6 convert_element_type.209
  694.3 35.9 %reduce-scatter.7.cloned.1.call-done = bf16[128,1024]{1,0:T(8,128)(2,1)} async-done(((bf16[1024,1024]{1,0:T(8,128)(2,1)}), bf16[128,1024]{1,0:T(8,128)(2,1)}) %reduce-scatter.7.cloned.1.call-update) | async-done | bytes 262160
  730.2 1.8 copy.150
  731.9 3.8 copy.178
  (131 shorter events, 25.1 us)
Async XLA Ops:
  11.3 36.5 %all-to-all-start = ((bf16[128,8,1024]{0,2,1:T(8,128)(2,1)}), bf16[128,8,1024]{0,2,1:T(8,128)(2,1)S(1)}, u32[]{:S(2)}, u32[]{:S(2)}) async-start(bf16[128,8,1024]{0,2,1:T(8,128)(2,1)} %bitcast.318), calls=%async_computation | async-start | bytes 4194304 | tf_op jit(solution)/shard_map/all_to_all | solution.py:127
  19.3 135.6 %reduce-scatter.5.cloned.1.call-start = ((), (), s32[]{:S(2)}) async-start(), calls=%async_computation.3 | async-start | bytes 7077888 | tf_op jit(solution)/shard_map/reduce_scatter | solution.py:129
  59.0 0.7 copy-start.18
  59.0 528.8 %all-gather.2.cloned.1.call-start = ((), (), s32[]{:S(2)}) async-start(), calls=%async_computation.4 | async-start | bytes 3538944 | tf_op jit(solution)/shard_map/all_gather | solution.py:176
  155.7 4.3 collective-permute-start
  158.3 2.0 copy-start.11
  159.7 1.0 copy-start.10
  162.6 49.0 %collective-permute-start.1 = (f32[2,2,2,128,512]{4,3,1,2,0:T(8,128)}, f32[2,2,2,128,512]{4,3,1,2,0:T(8,128)}, u32[]{:S(2)}, u32[]{:S(2)}) collective-permute-start(f32[2,2,2,128,512]{4,3,1,2,0:T(8,128)} %pad_maximum_fusion), channel_id=1, source_target_pairs={{0,64},{16,80},{32,96},{48,112},{64,0},{80,16},{96,32},{112,48},{1... | collective-permute-start | bytes 6291464 | tf_op jit(solution)/shard_map/ppermute | solution.py:9
  214.0 4.5 copy-start
  214.0 4.5 copy-start.2
  218.5 45.3 %collective-permute-start.2 = (f32[2,2,2,128,512]{4,3,1,2,0:T(8,128)}, f32[2,2,2,128,512]{4,3,1,2,0:T(8,128)}, u32[]{:S(2)}, u32[]{:S(2)}) collective-permute-start(f32[2,2,2,128,512]{4,3,1,2,0:T(8,128)} %maximum_select_fusion), channel_id=1, source_target_pairs={{0,32},{16,48},{32,0},{48,16},{64,96},{80,112},{96,64},{112,80},{1... | collective-permute-start | bytes 6291464 | tf_op jit(solution)/shard_map/ppermute | solution.py:9
  267.6 1.2 copy-start.1
  267.6 1.5 copy-start.3
  274.0 45.9 %collective-permute-start.3 = (f32[2,2,2,128,512]{4,3,1,2,0:T(8,128)}, f32[2,2,2,128,512]{4,3,1,2,0:T(8,128)S(1)}, u32[]{:S(2)}, u32[]{:S(2)}) collective-permute-start(f32[2,2,2,128,512]{4,3,1,2,0:T(8,128)} %maximum_select_fusion.1), channel_id=1, source_target_pairs={{0,16},{16,0},{32,48},{48,32},{64,80},{80,64},{96,112},{112,96},{1... | collective-permute-start | bytes 6291464 | tf_op jit(solution)/shard_map/ppermute | solution.py:9
  276.3 48.3 %copy-start.13 = (f32[2,128]{1,0:T(2,128)}, f32[2,128]{1,0:T(2,128)S(1)}, u32[]{:S(2)}) copy-start(f32[2,128]{1,0:T(2,128)S(1)} %get-tuple-element.80) | copy-start | bytes 3076
  276.3 48.3 %copy-start.15 = (f32[2,128]{1,0:T(2,128)}, f32[2,128]{1,0:T(2,128)S(1)}, u32[]{:S(2)}) copy-start(f32[2,128]{1,0:T(2,128)S(1)} %get-tuple-element.81) | copy-start | bytes 3076
  276.3 59.5 %copy-start.19 = (f32[2,128]{1,0:T(2,128)}, f32[2,128]{1,0:T(2,128)S(1)}, u32[]{:S(2)}) copy-start(f32[2,128]{1,0:T(2,128)S(1)} %get-tuple-element.78) | copy-start | bytes 3076
  276.3 59.5 %copy-start.21 = (f32[2,128]{1,0:T(2,128)}, f32[2,128]{1,0:T(2,128)S(1)}, u32[]{:S(2)}) copy-start(f32[2,128]{1,0:T(2,128)S(1)} %get-tuple-element.79) | copy-start | bytes 3076
  330.8 2.1 copy-start.4
  332.8 1.0 copy-start.6
  337.0 11.0 %collective-permute-start.4 = (bf16[2,1,2,128,512]{4,3,2,1,0:T(8,128)(2,1)S(1)}, bf16[2,1,2,128,512]{4,3,2,1,0:T(8,128)(2,1)S(1)}, u32[]{:S(2)}, u32[]{:S(2)}) collective-permute-start(bf16[2,1,2,128,512]{4,3,2,1,0:T(8,128)(2,1)S(1)} %fusion.32), channel_id=1, source_target_pairs={{0,16},{16,0},{32,48},{48,32},{64,80},{80,64},{96,112},{112,96},{1... | collective-permute-start | bytes 1572872 | tf_op jit(solution)/shard_map/ppermute | solution.py:9
  348.7 10.9 %collective-permute-start.5 = (bf16[2,1,2,128,512]{4,3,2,1,0:T(8,128)(2,1)S(1)}, bf16[2,1,2,128,512]{4,3,2,1,0:T(8,128)(2,1)S(1)}, u32[]{:S(2)}, u32[]{:S(2)}) collective-permute-start(bf16[2,1,2,128,512]{4,3,2,1,0:T(8,128)(2,1)S(1)} %get-tuple-element.17), channel_id=1, source_target_pairs={{0,32},{16,48},{32,0},{48,16},{64,96},{80,112},{96,64},{112,80},{1... | collective-permute-start | bytes 1572872 | tf_op jit(solution)/shard_map/ppermute | solution.py:9
  359.8 2.4 copy-start.9
  361.0 12.3 %collective-permute-start.6 = (bf16[2,1,2,128,512]{4,3,2,1,0:T(8,128)(2,1)}, bf16[2,1,2,128,512]{4,3,2,1,0:T(8,128)(2,1)S(1)}, u32[]{:S(2)}, u32[]{:S(2)}) collective-permute-start(bf16[2,1,2,128,512]{4,3,2,1,0:T(8,128)(2,1)} %get-tuple-element.15), channel_id=1, source_target_pairs={{0,64},{16,80},{32,96},{48,112},{64,0},{80,16},{96,32},{112,48},{1... | collective-permute-start | bytes 1572872 | tf_op jit(solution)/shard_map/ppermute | solution.py:9
  374.0 0.7 copy-start.17
  375.8 23.2 %collective-permute-start.7 = (f32[2,1,2,128,512]{4,3,2,1,0:T(8,128)S(1)}, f32[2,1,2,128,512]{4,3,2,1,0:T(8,128)S(1)}, u32[]{:S(2)}, u32[]{:S(2)}) collective-permute-start(f32[2,1,2,128,512]{4,3,2,1,0:T(8,128)S(1)} %pad_maximum_fusion.3), channel_id=1, source_target_pairs={{0,64},{16,80},{32,96},{48,112},{64,0},{80,16},{96,32},{112,48},{1... | collective-permute-start | bytes 3145736 | tf_op jit(solution)/shard_map/ppermute | solution.py:9
  399.7 15.6 %collective-permute-start.8 = (f32[2,1,2,128,512]{4,3,2,1,0:T(8,128)S(1)}, f32[2,1,2,128,512]{4,3,2,1,0:T(8,128)S(1)}, u32[]{:S(2)}, u32[]{:S(2)}) collective-permute-start(f32[2,1,2,128,512]{4,3,2,1,0:T(8,128)S(1)} %maximum_select_fusion.3), channel_id=1, source_target_pairs={{0,32},{16,48},{32,0},{48,16},{64,96},{80,112},{96,64},{112,80},{1... | collective-permute-start | bytes 3145736 | tf_op jit(solution)/shard_map/ppermute | solution.py:9
  416.7 17.2 %collective-permute-start.9 = (f32[2,1,2,128,512]{4,3,2,1,0:T(8,128)S(1)}, f32[2,1,2,128,512]{4,3,2,1,0:T(8,128)S(1)}, u32[]{:S(2)}, u32[]{:S(2)}) collective-permute-start(f32[2,1,2,128,512]{4,3,2,1,0:T(8,128)S(1)} %maximum_select_fusion.4), channel_id=1, source_target_pairs={{0,16},{16,0},{32,48},{48,32},{64,80},{80,64},{96,112},{112,96},{1... | collective-permute-start | bytes 3145736 | tf_op jit(solution)/shard_map/ppermute | solution.py:9
  434.3 0.7 copy-start.14
  434.3 0.7 copy-start.16
  435.0 3.6 copy-start.5
  435.0 3.6 copy-start.7
  442.8 1.3 copy-start.20
  442.8 1.3 copy-start.22
  446.0 16.6 %collective-permute-start.10 = (bf16[2,2,2,128,512]{4,3,1,2,0:T(8,128)(2,1)S(1)}, bf16[2,2,2,128,512]{4,3,1,2,0:T(8,128)(2,1)S(1)}, u32[]{:S(2)}, u32[]{:S(2)}) collective-permute-start(bf16[2,2,2,128,512]{4,3,1,2,0:T(8,128)(2,1)S(1)} %fusion.3), channel_id=1, source_target_pairs={{0,16},{16,0},{32,48},{48,32},{64,80},{80,64},{96,112},{112,96},{1... | collective-permute-start | bytes 3145736 | tf_op jit(solution)/shard_map/ppermute | solution.py:9
  464.1 14.9 %collective-permute-start.11 = (bf16[2,2,2,128,512]{4,3,1,2,0:T(8,128)(2,1)S(1)}, bf16[2,2,2,128,512]{4,3,1,2,0:T(8,128)(2,1)S(1)}, u32[]{:S(2)}, u32[]{:S(2)}) collective-permute-start(bf16[2,2,2,128,512]{4,3,1,2,0:T(8,128)(2,1)S(1)} %get-tuple-element.10), channel_id=1, source_target_pairs={{0,32},{16,48},{32,0},{48,16},{64,96},{80,112},{96,64},{112,80},{1... | collective-permute-start | bytes 3145736 | tf_op jit(solution)/shard_map/ppermute | solution.py:9
  480.5 30.1 %collective-permute-start.12 = (bf16[2,2,2,128,512]{4,3,1,2,0:T(8,128)(2,1)S(1)}, bf16[2,2,2,128,512]{4,3,1,2,0:T(8,128)(2,1)S(1)}, u32[]{:S(2)}, u32[]{:S(2)}) collective-permute-start(bf16[2,2,2,128,512]{4,3,1,2,0:T(8,128)(2,1)S(1)} %get-tuple-element.8), channel_id=1, source_target_pairs={{0,64},{16,80},{32,96},{48,112},{64,0},{80,16},{96,32},{112,48},{1... | collective-permute-start | bytes 3145736 | tf_op jit(solution)/shard_map/ppermute | solution.py:9
  512.6 7.4 copy-start.12
  512.8 7.1 collective-permute-start.13
  519.9 67.8 %copy-start.8 = (bf16[8,128,1024]{2,1,0:T(8,128)(2,1)S(1)}, bf16[8,128,1024]{2,1,0:T(8,128)(2,1)}, u32[]{:S(2)}) copy-start(bf16[8,128,1024]{2,1,0:T(8,128)(2,1)} %copy.91) | copy-start | bytes 6291460
  521.2 171.4 %all-reduce.5.cloned.1.call-start = ((), (), s32[]{:S(2)}) async-start(), calls=%async_computation.6 | async-start | bytes 6553600 | tf_op jit(solution)/shard_map/psum | solution.py:187
  599.3 130.9 %reduce-scatter.7.cloned.1.call-start = ((), (), s32[]{:S(2)}) async-start(), calls=%async_computation.5 | async-start | bytes 2359296
Sparse Core Ops, SparseCore 0:
  59.1 95.7 reduce-scatter.4
  521.3 66.4 all-gather.1
  599.4 93.1 all-reduce.4
  695.6 34.5 reduce-scatter.6
where the time goes:
time: 751 us; the launch traced here: 742 us
  waiting for transfers between devices  556 us (74%)
  starting transfers between devices  56.6 us (8%)
  matrix products  43.9 us (6%)
  other arithmetic  39.1 us (5%)
  local copies, waits for them, and re-layouts  31.3 us (4%)
  between operations  15.8 us (2%)
    ppermute x12, waiting for transfers between devices, partner_2(): lax.ppermute(shard, axis, [(i, i ^ 1 << stride) for i in range(lax.axis_s...  245 us
    reduce_scatter x1, waiting for transfers between devices, local(): lax.psum_scatter(jnp.dot(spread, flat_weight, preferred_element_type=jnp....  95.1 us
    psum x1, waiting for transfers between devices, local(): lax.psum((weight_total * grad_scale).astype(jnp.bfloat16), 'dp')  84.1 us
    all_gather x1, waiting for transfers between devices, local(): shard_rows = lax.all_gather(d_projected, 'seq', axis=0, tiled=True)  65.9 us
    ppermute x12, starting transfers between devices, partner_2(): lax.ppermute(shard, axis, [(i, i ^ 1 << stride) for i in range(lax.axis_s...  44.5 us
    unnamed x5, waiting for transfers between devices  36 us
    all_to_all x1, waiting for transfers between devices, local(): lax.all_to_all(tokens[0], 'seq', split_axis=1, concat_axis=0, tiled=True)  23.8 us
    unnamed x53, local copies, waits for them, and re-layouts  20 us
  transfers between devices with their start and end apart: 19, of which 18 were waited for; matrix products, arithmetic and copies ran while one was open for 3% of the time, Pallas kernels for 0%

commit v1 on v0

--- a/solution.py
+++ b/solution.py
@@ -3,6 +3,10 @@
 import jax.numpy as jnp
 from jax import lax
 from jax.sharding import PartitionSpec as P
+
+
+def drive_roots(sheet):
+    return jnp.sum(lax.all_gather(sheet, "dp"), 0)
 
 
 def partner_2(shard, axis, stride):
@@ -184,7 +188,7 @@
         token_block.astype(jnp.bfloat16), "chan", scatter_dimension=1, tiled=True
     )[None]
     weight_sum, filter_sum = (
-        lax.psum((weight_total * grad_scale).astype(jnp.bfloat16), "dp").astype(jnp.float32),
+        drive_roots((weight_total * grad_scale).astype(jnp.bfloat16)).astype(jnp.float32),
         lax.psum(filter_part.astype(jnp.bfloat16), "dp").astype(jnp.float32),
     )
     grad_weight = weight_sum.astype(jnp.bfloat16).reshape(slab_rows, 3, chan_cols)

time: 751 us -> 788 us (1.049)
  other arithmetic: 39.1 us -> 57.2 us
  waiting for transfers between devices: 556 us -> 565 us
  local copies, waits for them, and re-layouts: 31.3 us -> 39.9 us
    all_gather x0 -> x1, waiting for transfers between devices: none -> 82.1 us  [drive_roots(): return jnp.sum(lax.all_gather(sheet, 'dp'), 0)]
    psum x1, waiting for transfers between devices: 84.1 us -> 11.6 us  [local(): lax.psum(filter_part.astype(jnp.bfloat16), 'dp').astype(jnp.float32)]
    reduce_sum x0 -> x1, other arithmetic: none -> 18.2 us  [drive_roots(): return jnp.sum(lax.all_gather(sheet, 'dp'), 0)]
    all_gather x0 -> x1, local copies, waits for them, and re-layouts: none -> 11.1 us  [drive_roots(): return jnp.sum(lax.all_gather(sheet, 'dp'), 0)]
    unnamed x5 -> x6, waiting for transfers between devices: 36 us -> 35.3 us
  transfers between devices with their start and end apart: 19 -> 20, of which waited for: 18 -> 19; matrix products, arithmetic and copies ran while one was open for 3% -> 4% of each run, Pallas kernels for 0% -> 0%
where the time goes in v1:
time: 788 us; the launch traced here: 778 us
  waiting for transfers between devices  565 us (72%)
  other arithmetic  57.2 us (7%)
  starting transfers between devices  56.6 us (7%)
  matrix products  43.9 us (6%)
  local copies, waits for them, and re-layouts  39.9 us (5%)
  between operations  16 us (2%)
    ppermute x12, waiting for transfers between devices, partner_2(): lax.ppermute(shard, axis, [(i, i ^ 1 << stride) for i in range(lax.axis_s...  245 us
    reduce_scatter x1, waiting for transfers between devices, local(): lax.psum_scatter(jnp.dot(spread, flat_weight, preferred_element_type=jnp....  95.4 us
    all_gather x1, waiting for transfers between devices, drive_roots(): return jnp.sum(lax.all_gather(sheet, 'dp'), 0)  82.1 us
    all_gather x1, waiting for transfers between devices, local(): shard_rows = lax.all_gather(d_projected, 'seq', axis=0, tiled=True)  66.1 us
    ppermute x12, starting transfers between devices, partner_2(): lax.ppermute(shard, axis, [(i, i ^ 1 << stride) for i in range(lax.axis_s...  44.4 us
    unnamed x6, waiting for transfers between devices  35.3 us
    all_to_all x1, waiting for transfers between devices, local(): lax.all_to_all(tokens[0], 'seq', split_axis=1, concat_axis=0, tiled=True)  23.8 us
    unnamed x53, local copies, waits for them, and re-layouts  22.2 us
  transfers between devices with their start and end apart: 20, of which 19 were waited for; matrix products, arithmetic and copies ran while one was open for 4% of the time, Pallas kernels for 0%

profile of v1, /device:TPU:0, one launch (start us, length us, event | category | flops | bytes accessed | tf_op | source)
XLA Modules:
  0.0 778.4 jit_solution(3475664948657681862)
XLA Ops:
  7.2 4.1 copy.89
  11.2 8.0 %all-to-all-start = ((bf16[128,8,1024]{0,2,1:T(8,128)(2,1)}), bf16[128,8,1024]{0,2,1:T(8,128)(2,1)S(1)}, u32[]{:S(2)}, u32[]{:S(2)}) async-start(bf16[128,8,1024]{0,2,1:T(8,128)(2,1)} %bitcast.321), calls=%async_computation | async-start | bytes 4194304 | tf_op jit(solution)/shard_map/all_to_all | solution.py:131
  19.3 4.6 copy.91
  24.0 23.8 %all-to-all-done = bf16[128,8,1024]{0,2,1:T(8,128)(2,1)S(1)} async-done(((bf16[128,8,1024]{0,2,1:T(8,128)(2,1)}), bf16[128,8,1024]{0,2,1:T(8,128)(2,1)S(1)}, u32[]{:S(2)}, u32[]{:S(2)}) %all-to-all-start) | async-done | bytes 2097184 | tf_op jit(solution)/shard_map/all_to_all | solution.py:131
  47.8 2.6 copy.90
  50.4 8.6 %fusion.205 = f32[1024,1536]{1,0:T(8,128)} fusion(bf16[1024,1024]{1,0:T(8,128)(2,1)} %bitcast.329, bf16[1024,1536]{0,1:T(8,128)(2,1)} %bitcast.326), kind=kOutput, calls=%fused_computation.317 | convolution fusion | flops 3221225472 | bytes 11534336 | tf_op jit(solution)/shard_map/dot_general | solution.py:134
  59.7 95.4 %reduce-scatter.5.cloned.1.call-done = f32[128,1536]{1,0:T(8,128)} async-done(((f32[1024,1536]{1,0:T(8,128)}), f32[128,1536]{1,0:T(8,128)}) %reduce-scatter.5.cloned.1.call-update) | async-done | bytes 786448 | tf_op jit(solution)/shard_map/reduce_scatter | solution.py:133
  155.9 2.4 collective-permute-start
  158.6 1.4 copy.92
  161.3 1.6 pad_maximum_fusion
  162.9 4.8 collective-permute-start.1
  167.9 44.0 %collective-permute-done.1 = f32[2,2,2,128,512]{4,3,1,2,0:T(8,128)} collective-permute-done((f32[2,2,2,128,512]{4,3,1,2,0:T(8,128)}, f32[2,2,2,128,512]{4,3,1,2,0:T(8,128)}, u32[]{:S(2)}, u32[]{:S(2)}) %collective-permute-start.1) | collective-permute-done | bytes 2097184 | tf_op jit(solution)/shard_map/ppermute | solution.py:13
  211.9 2.1 fusion.184
  214.3 4.5 maximum_select_fusion
  218.8 1.9 collective-permute-start.2
  220.9 43.2 %collective-permute-done.2 = f32[2,2,2,128,512]{4,3,1,2,0:T(8,128)} collective-permute-done((f32[2,2,2,128,512]{4,3,1,2,0:T(8,128)}, f32[2,2,2,128,512]{4,3,1,2,0:T(8,128)}, u32[]{:S(2)}, u32[]{:S(2)}) %collective-permute-start.2) | collective-permute-done | bytes 2097184 | tf_op jit(solution)/shard_map/ppermute | solution.py:13
  264.1 3.8 fusion.213
  269.4 4.9 maximum_select_fusion.1
  274.3 2.2 collective-permute-start.3
  276.7 43.6 %collective-permute-done.3 = f32[2,2,2,128,512]{4,3,1,2,0:T(8,128)S(1)} collective-permute-done((f32[2,2,2,128,512]{4,3,1,2,0:T(8,128)}, f32[2,2,2,128,512]{4,3,1,2,0:T(8,128)S(1)}, u32[]{:S(2)}, u32[]{:S(2)}) %collective-permute-start.3) | collective-permute-done | bytes 2097184 | tf_op jit(solution)/shard_map/ppermute | solution.py:13
  320.2 2.1 sub.247
  322.6 2.4 maximum_select_fusion.2
  325.3 1.9 fusion.27
  327.2 1.9 fusion.31
  329.2 2.0 fusion.6
  331.1 2.0 fusion.8
  335.0 1.3 fusion.13
  337.5 2.2 collective-permute-start.4
  339.8 8.7 %collective-permute-done.4 = bf16[2,1,2,128,512]{4,3,2,1,0:T(8,128)(2,1)S(1)} collective-permute-done((bf16[2,1,2,128,512]{4,3,2,1,0:T(8,128)(2,1)S(1)}, bf16[2,1,2,128,512]{4,3,2,1,0:T(8,128)(2,1)S(1)}, u32[]{:S(2)}, u32[]{:S(2)}) %collective-permute-start.4) | collective-permute-done | bytes 524320 | tf_op jit(solution)/shard_map/ppermute | solution.py:13
  349.2 1.8 collective-permute-start.5
  351.3 8.7 %collective-permute-done.5 = bf16[2,1,2,128,512]{4,3,2,1,0:T(8,128)(2,1)S(1)} collective-permute-done((bf16[2,1,2,128,512]{4,3,2,1,0:T(8,128)(2,1)S(1)}, bf16[2,1,2,128,512]{4,3,2,1,0:T(8,128)(2,1)S(1)}, u32[]{:S(2)}, u32[]{:S(2)}) %collective-permute-start.5) | collective-permute-done | bytes 524320 | tf_op jit(solution)/shard_map/ppermute | solution.py:13
  360.2 1.2 fusion.190
  362.9 10.8 %collective-permute-done.6 = bf16[2,1,2,128,512]{4,3,2,1,0:T(8,128)(2,1)S(1)} collective-permute-done((bf16[2,1,2,128,512]{4,3,2,1,0:T(8,128)(2,1)}, bf16[2,1,2,128,512]{4,3,2,1,0:T(8,128)(2,1)S(1)}, u32[]{:S(2)}, u32[]{:S(2)}) %collective-permute-start.6) | collective-permute-done | bytes 524320 | tf_op jit(solution)/shard_map/ppermute | solution.py:13
  376.3 22.9 %collective-permute-done.7 = f32[2,1,2,128,512]{4,3,2,1,0:T(8,128)S(1)} collective-permute-done((f32[2,1,2,128,512]{4,3,2,1,0:T(8,128)S(1)}, f32[2,1,2,128,512]{4,3,2,1,0:T(8,128)S(1)}, u32[]{:S(2)}, u32[]{:S(2)}) %collective-permute-start.7) | collective-permute-done | bytes 1048608 | tf_op jit(solution)/shard_map/ppermute | solution.py:13
  400.0 3.0 collective-permute-start.8
  403.0 12.8 %collective-permute-done.8 = f32[2,1,2,128,512]{4,3,2,1,0:T(8,128)S(1)} collective-permute-done((f32[2,1,2,128,512]{4,3,2,1,0:T(8,128)S(1)}, f32[2,1,2,128,512]{4,3,2,1,0:T(8,128)S(1)}, u32[]{:S(2)}, u32[]{:S(2)}) %collective-permute-start.8) | collective-permute-done | bytes 1048608 | tf_op jit(solution)/shard_map/ppermute | solution.py:13
  417.2 4.2 collective-permute-start.9
  421.3 12.8 %collective-permute-done.9 = f32[2,1,2,128,512]{4,3,2,1,0:T(8,128)S(1)} collective-permute-done((f32[2,1,2,128,512]{4,3,2,1,0:T(8,128)S(1)}, f32[2,1,2,128,512]{4,3,2,1,0:T(8,128)S(1)}, u32[]{:S(2)}, u32[]{:S(2)}) %collective-permute-start.9) | collective-permute-done | bytes 1048608 | tf_op jit(solution)/shard_map/ppermute | solution.py:13
  438.8 1.3 fusion.50
  440.4 1.3 fusion.21
  441.7 1.3 fusion.25
  443.0 1.3 convolution_add_fusion
  444.4 1.6 fusion.20
  446.1 3.8 collective-permute-start.10
  450.2 12.6 %collective-permute-done.10 = bf16[2,2,2,128,512]{4,3,1,2,0:T(8,128)(2,1)S(1)} collective-permute-done((bf16[2,2,2,128,512]{4,3,1,2,0:T(8,128)(2,1)S(1)}, bf16[2,2,2,128,512]{4,3,1,2,0:T(8,128)(2,1)S(1)}, u32[]{:S(2)}, u32[]{:S(2)}) %collective-permute-start.10) | collective-permute-done | bytes 1048608 | tf_op jit(solution)/shard_map/ppermute | solution.py:13
  464.2 2.0 collective-permute-start.11
  466.6 12.5 %collective-permute-done.11 = bf16[2,2,2,128,512]{4,3,1,2,0:T(8,128)(2,1)S(1)} collective-permute-done((bf16[2,2,2,128,512]{4,3,1,2,0:T(8,128)(2,1)S(1)}, bf16[2,2,2,128,512]{4,3,1,2,0:T(8,128)(2,1)S(1)}, u32[]{:S(2)}, u32[]{:S(2)}) %collective-permute-start.11) | collective-permute-done | bytes 1048608 | tf_op jit(solution)/shard_map/ppermute | solution.py:13
  480.5 17.3 %collective-permute-start.12 = (bf16[2,2,2,128,512]{4,3,1,2,0:T(8,128)(2,1)S(1)}, bf16[2,2,2,128,512]{4,3,1,2,0:T(8,128)(2,1)S(1)}, u32[]{:S(2)}, u32[]{:S(2)}) collective-permute-start(bf16[2,2,2,128,512]{4,3,1,2,0:T(8,128)(2,1)S(1)} %get-tuple-element.18), channel_id=1, source_target_pairs={{0,64},{16,80},{32,96},{48,112},{64,0},{80,16},{96,32},{112,48},{1... | collective-permute-start | bytes 3145736 | tf_op jit(solution)/shard_map/ppermute | solution.py:13
  498.3 12.4 %collective-permute-done.12 = bf16[2,2,2,128,512]{4,3,1,2,0:T(8,128)(2,1)S(1)} collective-permute-done((bf16[2,2,2,128,512]{4,3,1,2,0:T(8,128)(2,1)S(1)}, bf16[2,2,2,128,512]{4,3,1,2,0:T(8,128)(2,1)S(1)}, u32[]{:S(2)}, u32[]{:S(2)}) %collective-permute-start.12) | collective-permute-done | bytes 1048608 | tf_op jit(solution)/shard_map/ppermute | solution.py:13
  512.7 1.3 collective-permute-start.13
  514.0 5.8 collective-permute-done.13
  521.9 66.1 %all-gather.4.cloned.1.call-done = bf16[1024,1536]{0,1:T(8,128)(2,1)} async-done(((bf16[128,1536]{0,1:T(8,128)(2,1)}), bf16[1024,1536]{0,1:T(8,128)(2,1)}) %all-gather.4.cloned.1.call-update) | async-done | bytes 3145744 | tf_op jit(solution)/shard_map/all_gather | solution.py:180
  588.0 6.3 convolution_convert_fusion
  594.4 2.6 copy.148
  597.3 1.3 copy-done.8
  598.5 6.7 fusion
  605.2 11.6 %all-reduce.4.cloned.1.call-done = bf16[128,512]{1,0:T(8,128)(2,1)} async-done(((bf16[128,512]{1,0:T(8,128)(2,1)}), bf16[128,512]{1,0:T(8,128)(2,1)}) %all-reduce.4.cloned.1.call-update) | async-done | bytes 131088 | tf_op jit(solution)/shard_map/psum | solution.py:192
  616.8 1.6 convert_element_type.211
  618.5 35.2 %reduce-scatter.7.cloned.1.call-done = bf16[128,1024]{1,0:T(8,128)(2,1)} async-done(((bf16[1024,1024]{1,0:T(8,128)(2,1)}), bf16[128,1024]{1,0:T(8,128)(2,1)}) %reduce-scatter.7.cloned.1.call-update) | async-done | bytes 262160
  653.6 1.8 copy.149
  655.4 82.1 %all-gather.6.cloned.1.call-done = bf16[2048,1536]{0,1:T(8,128)(2,1)} async-done(((bf16[1024,1536]{0,1:T(8,128)(2,1)}), bf16[2048,1536]{0,1:T(8,128)(2,1)}) %all-gather.6.cloned.1.call-update) | async-done | bytes 6291472 | tf_op jit(solution)/shard_map/all_gather | solution.py:9
  737.5 11.1 %reshape.746 = bf16[2,1024,1536]{1,0,2:T(2,128)(2,1)} reshape(bf16[2048,1536]{0,1:T(8,128)(2,1)} %all-gather.6.cloned.1.call-done) | data formatting | bytes 12582912 | tf_op jit(solution)/shard_map/all_gather | solution.py:9
  748.6 18.2 %reduce_sum.12 = bf16[1024,1536]{0,1:T(8,128)(2,1)} reduce(bf16[2,1024,1536]{1,0,2:T(2,128)(2,1)} %reshape.746, bf16[]{:T(256)} %constant.275.clone.1), dimensions={0}, to_apply=%region_2.3 | reduce | flops 1572864 | bytes 9437186 | tf_op jit(solution)/shard_map/reduce_sum | solution.py:9
  766.8 4.6 copy.117
  (135 shorter events, 28.7 us)
Async XLA Ops:
  11.2 36.5 %all-to-all-start = ((bf16[128,8,1024]{0,2,1:T(8,128)(2,1)}), bf16[128,8,1024]{0,2,1:T(8,128)(2,1)S(1)}, u32[]{:S(2)}, u32[]{:S(2)}) async-start(bf16[128,8,1024]{0,2,1:T(8,128)(2,1)} %bitcast.321), calls=%async_computation | async-start | bytes 4194304 | tf_op jit(solution)/shard_map/all_to_all | solution.py:131
  19.3 135.9 %reduce-scatter.5.cloned.1.call-start = ((), (), s32[]{:S(2)}) async-start(), calls=%async_computation.3 | async-start | bytes 7077888 | tf_op jit(solution)/shard_map/reduce_scatter | solution.py:133
  59.0 0.7 copy-start.18
  59.0 529.0 %all-gather.4.cloned.1.call-start = ((), (), s32[]{:S(2)}) async-start(), calls=%async_computation.4 | async-start | bytes 3538944 | tf_op jit(solution)/shard_map/all_gather | solution.py:180
  155.9 4.3 collective-permute-start
  158.6 2.0 copy-start.11
  160.0 1.0 copy-start.10
  162.9 49.0 %collective-permute-start.1 = (f32[2,2,2,128,512]{4,3,1,2,0:T(8,128)}, f32[2,2,2,128,512]{4,3,1,2,0:T(8,128)}, u32[]{:S(2)}, u32[]{:S(2)}) collective-permute-start(f32[2,2,2,128,512]{4,3,1,2,0:T(8,128)} %pad_maximum_fusion), channel_id=1, source_target_pairs={{0,64},{16,80},{32,96},{48,112},{64,0},{80,16},{96,32},{112,48},{1... | collective-permute-start | bytes 6291464 | tf_op jit(solution)/shard_map/ppermute | solution.py:13
  214.3 4.5 copy-start
  214.3 4.5 copy-start.2
  218.8 45.3 %collective-permute-start.2 = (f32[2,2,2,128,512]{4,3,1,2,0:T(8,128)}, f32[2,2,2,128,512]{4,3,1,2,0:T(8,128)}, u32[]{:S(2)}, u32[]{:S(2)}) collective-permute-start(f32[2,2,2,128,512]{4,3,1,2,0:T(8,128)} %maximum_select_fusion), channel_id=1, source_target_pairs={{0,32},{16,48},{32,0},{48,16},{64,96},{80,112},{96,64},{112,80},{1... | collective-permute-start | bytes 6291464 | tf_op jit(solution)/shard_map/ppermute | solution.py:13
  267.9 1.2 copy-start.1
  267.9 1.5 copy-start.3
  274.3 46.0 %collective-permute-start.3 = (f32[2,2,2,128,512]{4,3,1,2,0:T(8,128)}, f32[2,2,2,128,512]{4,3,1,2,0:T(8,128)S(1)}, u32[]{:S(2)}, u32[]{:S(2)}) collective-permute-start(f32[2,2,2,128,512]{4,3,1,2,0:T(8,128)} %maximum_select_fusion.1), channel_id=1, source_target_pairs={{0,16},{16,0},{32,48},{48,32},{64,80},{80,64},{96,112},{112,96},{1... | collective-permute-start | bytes 6291464 | tf_op jit(solution)/shard_map/ppermute | solution.py:13
  276.6 48.3 %copy-start.13 = (f32[2,128]{1,0:T(2,128)}, f32[2,128]{1,0:T(2,128)S(1)}, u32[]{:S(2)}) copy-start(f32[2,128]{1,0:T(2,128)S(1)} %get-tuple-element.90) | copy-start | bytes 3076
  276.6 48.3 %copy-start.15 = (f32[2,128]{1,0:T(2,128)}, f32[2,128]{1,0:T(2,128)S(1)}, u32[]{:S(2)}) copy-start(f32[2,128]{1,0:T(2,128)S(1)} %get-tuple-element.91) | copy-start | bytes 3076
  276.6 59.7 %copy-start.19 = (f32[2,128]{1,0:T(2,128)}, f32[2,128]{1,0:T(2,128)S(1)}, u32[]{:S(2)}) copy-start(f32[2,128]{1,0:T(2,128)S(1)} %get-tuple-element.88) | copy-start | bytes 3076
  276.7 59.7 %copy-start.21 = (f32[2,128]{1,0:T(2,128)}, f32[2,128]{1,0:T(2,128)S(1)}, u32[]{:S(2)}) copy-start(f32[2,128]{1,0:T(2,128)S(1)} %get-tuple-element.89) | copy-start | bytes 3076
  331.1 2.1 copy-start.4
  333.1 1.0 copy-start.6
  337.5 11.0 %collective-permute-start.4 = (bf16[2,1,2,128,512]{4,3,2,1,0:T(8,128)(2,1)S(1)}, bf16[2,1,2,128,512]{4,3,2,1,0:T(8,128)(2,1)S(1)}, u32[]{:S(2)}, u32[]{:S(2)}) collective-permute-start(bf16[2,1,2,128,512]{4,3,2,1,0:T(8,128)(2,1)S(1)} %fusion.33), channel_id=1, source_target_pairs={{0,16},{16,0},{32,48},{48,32},{64,80},{80,64},{96,112},{112,96},{1... | collective-permute-start | bytes 1572872 | tf_op jit(solution)/shard_map/ppermute | solution.py:13
  349.2 10.8 %collective-permute-start.5 = (bf16[2,1,2,128,512]{4,3,2,1,0:T(8,128)(2,1)S(1)}, bf16[2,1,2,128,512]{4,3,2,1,0:T(8,128)(2,1)S(1)}, u32[]{:S(2)}, u32[]{:S(2)}) collective-permute-start(bf16[2,1,2,128,512]{4,3,2,1,0:T(8,128)(2,1)S(1)} %get-tuple-element.27), channel_id=1, source_target_pairs={{0,32},{16,48},{32,0},{48,16},{64,96},{80,112},{96,64},{112,80},{1... | collective-permute-start | bytes 1572872 | tf_op jit(solution)/shard_map/ppermute | solution.py:13
  360.2 2.4 copy-start.9
  361.5 12.2 %collective-permute-start.6 = (bf16[2,1,2,128,512]{4,3,2,1,0:T(8,128)(2,1)}, bf16[2,1,2,128,512]{4,3,2,1,0:T(8,128)(2,1)S(1)}, u32[]{:S(2)}, u32[]{:S(2)}) collective-permute-start(bf16[2,1,2,128,512]{4,3,2,1,0:T(8,128)(2,1)} %get-tuple-element.25), channel_id=1, source_target_pairs={{0,64},{16,80},{32,96},{48,112},{64,0},{80,16},{96,32},{112,48},{1... | collective-permute-start | bytes 1572872 | tf_op jit(solution)/shard_map/ppermute | solution.py:13
  374.4 0.7 copy-start.17
  376.2 23.0 %collective-permute-start.7 = (f32[2,1,2,128,512]{4,3,2,1,0:T(8,128)S(1)}, f32[2,1,2,128,512]{4,3,2,1,0:T(8,128)S(1)}, u32[]{:S(2)}, u32[]{:S(2)}) collective-permute-start(f32[2,1,2,128,512]{4,3,2,1,0:T(8,128)S(1)} %pad_maximum_fusion.3), channel_id=1, source_target_pairs={{0,64},{16,80},{32,96},{48,112},{64,0},{80,16},{96,32},{112,48},{1... | collective-permute-start | bytes 3145736 | tf_op jit(solution)/shard_map/ppermute | solution.py:13
  400.0 15.8 %collective-permute-start.8 = (f32[2,1,2,128,512]{4,3,2,1,0:T(8,128)S(1)}, f32[2,1,2,128,512]{4,3,2,1,0:T(8,128)S(1)}, u32[]{:S(2)}, u32[]{:S(2)}) collective-permute-start(f32[2,1,2,128,512]{4,3,2,1,0:T(8,128)S(1)} %maximum_select_fusion.3), channel_id=1, source_target_pairs={{0,32},{16,48},{32,0},{48,16},{64,96},{80,112},{96,64},{112,80},{1... | collective-permute-start | bytes 3145736 | tf_op jit(solution)/shard_map/ppermute | solution.py:13
  417.2 16.9 %collective-permute-start.9 = (f32[2,1,2,128,512]{4,3,2,1,0:T(8,128)S(1)}, f32[2,1,2,128,512]{4,3,2,1,0:T(8,128)S(1)}, u32[]{:S(2)}, u32[]{:S(2)}) collective-permute-start(f32[2,1,2,128,512]{4,3,2,1,0:T(8,128)S(1)} %maximum_select_fusion.4), channel_id=1, source_target_pairs={{0,16},{16,0},{32,48},{48,32},{64,80},{80,64},{96,112},{112,96},{1... | collective-permute-start | bytes 3145736 | tf_op jit(solution)/shard_map/ppermute | solution.py:13
  434.5 0.7 copy-start.14
  434.5 0.7 copy-start.16
  435.2 3.6 copy-start.5
  435.2 3.6 copy-start.7
  443.0 1.3 copy-start.20
  443.0 1.3 copy-start.22
  446.1 16.6 %collective-permute-start.10 = (bf16[2,2,2,128,512]{4,3,1,2,0:T(8,128)(2,1)S(1)}, bf16[2,2,2,128,512]{4,3,1,2,0:T(8,128)(2,1)S(1)}, u32[]{:S(2)}, u32[]{:S(2)}) collective-permute-start(bf16[2,2,2,128,512]{4,3,1,2,0:T(8,128)(2,1)S(1)} %fusion.4), channel_id=1, source_target_pairs={{0,16},{16,0},{32,48},{48,32},{64,80},{80,64},{96,112},{112,96},{1... | collective-permute-start | bytes 3145736 | tf_op jit(solution)/shard_map/ppermute | solution.py:13
  464.2 14.9 %collective-permute-start.11 = (bf16[2,2,2,128,512]{4,3,1,2,0:T(8,128)(2,1)S(1)}, bf16[2,2,2,128,512]{4,3,1,2,0:T(8,128)(2,1)S(1)}, u32[]{:S(2)}, u32[]{:S(2)}) collective-permute-start(bf16[2,2,2,128,512]{4,3,1,2,0:T(8,128)(2,1)S(1)} %get-tuple-element.20), channel_id=1, source_target_pairs={{0,32},{16,48},{32,0},{48,16},{64,96},{80,112},{96,64},{112,80},{1... | collective-permute-start | bytes 3145736 | tf_op jit(solution)/shard_map/ppermute | solution.py:13
  480.5 30.1 %collective-permute-start.12 = (bf16[2,2,2,128,512]{4,3,1,2,0:T(8,128)(2,1)S(1)}, bf16[2,2,2,128,512]{4,3,1,2,0:T(8,128)(2,1)S(1)}, u32[]{:S(2)}, u32[]{:S(2)}) collective-permute-start(bf16[2,2,2,128,512]{4,3,1,2,0:T(8,128)(2,1)S(1)} %get-tuple-element.18), channel_id=1, source_target_pairs={{0,64},{16,80},{32,96},{48,112},{64,0},{80,16},{96,32},{112,48},{1... | collective-permute-start | bytes 3145736 | tf_op jit(solution)/shard_map/ppermute | solution.py:13
  512.5 7.4 copy-start.12
  512.7 7.1 collective-permute-start.13
  521.1 95.7 %all-reduce.4.cloned.1.call-start = ((), (), s32[]{:S(2)}) async-start(), calls=%async_computation.5 | async-start | bytes 262144 | tf_op jit(solution)/shard_map/psum | solution.py:192
  521.9 131.8 %reduce-scatter.7.cloned.1.call-start = ((), (), s32[]{:S(2)}) async-start(), calls=%async_computation.7 | async-start | bytes 2359296
  596.9 1.6 copy-start.8
  597.0 140.5 %all-gather.6.cloned.1.call-start = ((), (), s32[]{:S(2)}) async-start(), calls=%async_computation.6 | async-start | bytes 9437184 | tf_op jit(solution)/shard_map/all_gather | solution.py:9
Sparse Core Ops, SparseCore 0:
  59.1 95.9 reduce-scatter.4
  521.3 66.7 all-gather.3
  591.0 25.7 all-reduce.3
  619.1 34.5 reduce-scatter.6
  655.7 81.7 all-gather.5
